TPU v7x, 128 devices: a whole 4x4x4 slice. The times are simulated.
128 devices in a mesh: row: 8 (over x, core), col: 16 (over y, z).
Axes of the slice: x: 4, y: 4, z: 4, core: 2. Of those that a mesh axis runs over, the one named last changes fastest.
Arguments:
- density: float32 [768, 13, 4096], P(('row', 'col')), as said below
- pattern: int32 [768, 13], P(('row', 'col')), may hold values from 0 to 1, as said below
Outputs:
- purified: float32 [768, 13, 4096], P(('row', 'col'))
Inputs may be any that keep to these rules, and one draw needn't show every extreme that they name: `pattern`: slot 6 is 1 in every row; slot s of block row i equals slot 12 - s of block row (i + s - 6) modulo 768. `density`: the block at slot s of block row i is the transpose of the block at slot 12 - s of block row (i + s - 6) modulo 768; blocks are zero where pattern is 0.
All inputs are finite; a program needn't handle non-finite values.
Results may differ from a plain program's by a relative error of at most 0.0001.
Values sent between devices are 32-bit elements; how exact they have to be, the bound alone decides.
No kernel may reach another device: no remote copies, remote signals or barrier semaphores. Data moves between devices by JAX's collectives and lax.ppermute only.
A program may use at most 128 MiB of HBM per device.

v0:
```python
import jax
import jax.numpy as jnp
from jax import lax
from jax.experimental import pallas as pl
from jax.experimental.pallas import tpu as pltpu
from jax.sharding import PartitionSpec as P

BLK = 64
HALF = 6
SLOTS = 13
ROWS = 6
SUP = ROWS * BLK
LANES = 128
TILES = SUP // LANES
PACKED = 672
F32 = jnp.float32
BF16 = jnp.bfloat16


def lane_is_low(rows):
    return lax.broadcasted_iota(jnp.int32, (rows, LANES), 1) < BLK


def load_block(x_ref, row, slot):
    if slot < 0 or slot >= SLOTS:
        return jnp.zeros((BLK // 2, LANES), F32)
    return x_ref[row, slot, :].reshape(BLK // 2, LANES)


def even_odd_rows(left, right):
    low = lane_is_low(BLK // 2)
    even = jnp.where(low, left, pltpu.roll(right, BLK, 1))
    odd = jnp.where(low, pltpu.roll(left, BLK, 1), right)
    return even, odd


def store_pair(ref, lead, first_row, left, right):
    even, odd = even_odd_rows(left, right)
    ref[(*lead, pl.ds(first_row, BLK // 2, stride=2), slice(None))] = even
    ref[(*lead, pl.ds(first_row + 1, BLK // 2, stride=2), slice(None))] = odd


def split(x):
    hi = x.astype(BF16)
    return hi, (x - hi.astype(F32)).astype(BF16)


def dot(a, b):
    return jnp.dot(a, b, preferred_element_type=F32)


def dot3(ah, al, bh, bl):
    return dot(jnp.concatenate([ah, ah, al], 1), jnp.concatenate([bh, bl, bh], 0))


def mask_tile(pat_ref, row, tile):
    values = []
    for q in (2 * tile, 2 * tile + 1):
        slot = q - row
        values.append(pat_ref[row, slot].astype(F32) if 0 <= slot < SLOTS else jnp.float32(0.0))
    return jnp.where(lane_is_low(8), values[0], values[1])[:1]


def pack_kernel(x_ref, out_ref):
    first = 0
    for p in range(TILES):
        for row in (2 * p, 2 * p + 1):
            for q in range(p, TILES):
                if q == p and row % 2:
                    continue
                slot = 2 * q - row + HALF
                store_pair(out_ref, (), first, load_block(x_ref, row, slot), load_block(x_ref, row, slot + 1))
                first += BLK
    store_pair(out_ref, (), first, load_block(x_ref, 1, HALF), load_block(x_ref, 3, HALF))
    first += BLK
    out_ref[first : first + BLK // 2, :] = load_block(x_ref, 5, HALF)


def unpack(rec_ref, tri_ref):
    first = 0
    zeros = jnp.zeros((BLK, LANES), F32)
    for p in range(TILES):
        for row in (2 * p, 2 * p + 1):
            for q in range(p, TILES):
                if q == p and row % 2:
                    continue
                tri_ref[q, row * BLK : (row + 1) * BLK, :] = rec_ref[first : first + BLK, :]
                first += BLK
    corner = rec_ref[first : first + BLK, :]
    low = lane_is_low(BLK)
    tri_ref[0, BLK : 2 * BLK, :] = jnp.where(low, zeros, pltpu.roll(corner, BLK, 1))
    tri_ref[1, 3 * BLK : 4 * BLK, :] = jnp.where(low, zeros, corner)
    first += BLK
    last = rec_ref[first : first + BLK // 2, :]
    store_pair(tri_ref, (2,), 5 * BLK, jnp.zeros((BLK // 2, LANES), F32), last)


def unpack_split(rec_ref, tri_ref, hi_ref, lo_ref):
    unpack(rec_ref, tri_ref)
    shape = (LANES, LANES)
    corner = (lax.broadcasted_iota(jnp.int32, shape, 0) >= BLK) & (lax.broadcasted_iota(jnp.int32, shape, 1) < BLK)
    for p in range(TILES):
        for q in range(p, TILES):
            tile = tri_ref[q, p * LANES : (p + 1) * LANES, :]
            turned = tile.T
            here = (slice(p * LANES, (p + 1) * LANES), slice(q * LANES, (q + 1) * LANES))
            there = (here[1], here[0])
            if p == q:
                hi_ref[here], lo_ref[here] = split(jnp.where(corner, turned, tile))
            else:
                hi_ref[here], lo_ref[here] = split(tile)
                hi_ref[there], lo_ref[there] = split(turned)


def local_kernel(pat_ref, x_ref, xh_ref, xl_ref, th_ref, tl_ref, base_ref, part_ref, side_ref, nat_ref, sqh_ref, sql_ref):
    for row in range(ROWS):
        for tile in range(3 * TILES):
            slot = 2 * tile - row
            store_pair(nat_ref, (tile,), row * BLK, load_block(x_ref, row, slot), load_block(x_ref, row, slot + 1))
    for tile in range(3 * TILES):
        cols = slice(tile * LANES, (tile + 1) * LANES)
        xh_ref[:, cols], xl_ref[:, cols] = split(nat_ref[tile])
        th_ref[cols, :], tl_ref[cols, :] = split(nat_ref[tile].T)
    square = dot3(xh_ref[...], xl_ref[...], th_ref[...], tl_ref[...])
    for row in range(ROWS):
        rows = slice(row * BLK, (row + 1) * BLK)
        for tile in range(TILES):
            cols = slice(tile * LANES, (tile + 1) * LANES)
            kept = square[rows, cols] * mask_tile(pat_ref, row, TILES + tile)
            base_ref[rows, cols] = kept
            sqh_ref[rows, cols], sql_ref[rows, cols] = split(kept)
    dh, dl = xh_ref[:, SUP : 2 * SUP], xl_ref[:, SUP : 2 * SUP]
    for side, first in ((0, 0), (1, 2 * SUP)):
        cols = slice(first, first + SUP)
        part_ref[side] = dot3(dh, dl, xh_ref[:, cols], xl_ref[:, cols])
        side_ref[side] = dot3(sqh_ref[...], sql_ref[...], xh_ref[:, cols], xl_ref[:, cols])
    cube = dot3(sqh_ref[...], sql_ref[...], dh, dl)
    base_ref[...] = 3.0 * base_ref[...] - 2.0 * cube


def finish_kernel(
    pat_ref, prev_ref, next_ref, xh_ref, xl_ref, th_ref, tl_ref, base_ref, part_ref, side_ref,
    out_ref, tri_ref, dh_ref, dl_ref, eh_ref, el_ref, nat_ref,
):
    for side, rec_ref in ((0, prev_ref), (1, next_ref)):
        unpack_split(rec_ref, tri_ref.at[side], dh_ref.at[side], dl_ref.at[side])
    for side in (0, 1):
        cols = slice(2 * side * SUP, (2 * side + 1) * SUP)
        edge = part_ref[side] + dot3(xh_ref[:, cols], xl_ref[:, cols], dh_ref[side], dl_ref[side])
        for row in range(ROWS):
            rows = slice(row * BLK, (row + 1) * BLK)
            for t in range(TILES):
                tile = 2 * side * TILES + t
                lanes = slice(t * LANES, (t + 1) * LANES)
                kept = edge[rows, lanes] * mask_tile(pat_ref, row, tile)
                nat_ref[tile, rows, :] = 3.0 * kept
                lanes = slice(side * SUP + t * LANES, side * SUP + (t + 1) * LANES)
                eh_ref[rows, lanes], el_ref[rows, lanes] = split(kept)
    for side in (0, 1):
        cols = slice(side * SUP, (side + 1) * SUP)
        cube = side_ref[side] + dot3(eh_ref[:, cols], el_ref[:, cols], dh_ref[side], dl_ref[side])
        for t in range(TILES):
            tile = 2 * side * TILES + t
            nat_ref[tile] = nat_ref[tile] - 2.0 * cube[:, t * LANES : (t + 1) * LANES]
    turned_h = jnp.concatenate([th_ref[:SUP, :], th_ref[2 * SUP :, :]], 0)
    turned_l = jnp.concatenate([tl_ref[:SUP, :], tl_ref[2 * SUP :, :]], 0)
    cube = dot3(eh_ref[...], el_ref[...], turned_h, turned_l)
    for t in range(TILES):
        lanes = slice(t * LANES, (t + 1) * LANES)
        nat_ref[TILES + t] = base_ref[:, lanes] - 2.0 * cube[:, lanes]
    for row in range(ROWS):
        for tile in range(row // 2, (row + SLOTS - 1) // 2 + 1):
            mask = mask_tile(pat_ref, row, tile)
            even = nat_ref[tile, pl.ds(row * BLK, BLK // 2, stride=2), :] * mask
            odd = nat_ref[tile, pl.ds(row * BLK + 1, BLK // 2, stride=2), :] * mask
            left, right = even_odd_rows(even, odd)
            for slot, block in ((2 * tile - row, left), (2 * tile + 1 - row, right)):
                if 0 <= slot < SLOTS:
                    out_ref[row, slot, :] = block.reshape(BLK * BLK)


def from_behind(x, by):
    axes = ("row", "col")
    length = lax.axis_size(axes)
    return lax.ppermute(x, axes, [(i, (i + by) % length) for i in range(length)])


def shards(density, pattern):
    smem = pl.BlockSpec(memory_space=pltpu.SMEM)
    vmem = pl.BlockSpec(memory_space=pltpu.VMEM)
    packed = pl.pallas_call(
        pack_kernel, out_shape=jax.ShapeDtypeStruct((PACKED, LANES), F32), name="pack"
    )(density)
    prev = from_behind(packed, 1)
    following = from_behind(packed, -1)
    local = pl.pallas_call(
        local_kernel,
        name="local",
        in_specs=[smem, vmem],
        out_specs=[vmem] * 7,
        out_shape=[
            jax.ShapeDtypeStruct((SUP, 3 * SUP), BF16),
            jax.ShapeDtypeStruct((SUP, 3 * SUP), BF16),
            jax.ShapeDtypeStruct((3 * SUP, SUP), BF16),
            jax.ShapeDtypeStruct((3 * SUP, SUP), BF16),
            jax.ShapeDtypeStruct((SUP, SUP), F32),
            jax.ShapeDtypeStruct((2, SUP, SUP), F32),
            jax.ShapeDtypeStruct((2, SUP, SUP), F32),
        ],
        scratch_shapes=[
            pltpu.VMEM((3 * TILES, SUP, LANES), F32),
            pltpu.VMEM((SUP, SUP), BF16),
            pltpu.VMEM((SUP, SUP), BF16),
        ],
    )(pattern, density)
    return pl.pallas_call(
        finish_kernel,
        name="finish",
        in_specs=[smem] + [vmem] * 9,
        out_specs=vmem,
        out_shape=jax.ShapeDtypeStruct((ROWS, SLOTS, BLK * BLK), F32),
        scratch_shapes=[
            pltpu.VMEM((2, TILES, SUP, LANES), F32),
            pltpu.VMEM((2, SUP, SUP), BF16),
            pltpu.VMEM((2, SUP, SUP), BF16),
            pltpu.VMEM((SUP, 2 * SUP), BF16),
            pltpu.VMEM((SUP, 2 * SUP), BF16),
            pltpu.VMEM((3 * TILES, SUP, LANES), F32),
        ],
    )(pattern, prev, following, *local)


def solution(mesh):
    return jax.shard_map(
        shards,
        mesh=mesh,
        in_specs=(P(("row", "col"), None, None), P(("row", "col"), None)),
        out_specs=P(("row", "col"), None, None),
        check_vma=False,
    )
```

profile of v0, /device:TPU:1, one launch (start us, length us, event | category | flops | bytes accessed | tf_op | source)
XLA Modules:
  0.0 32.3 jit_solution(383760407650816957)
XLA Ops:
  0.0 2.3 %pack.1 = f32[672,128]{1,0:T(8,128)} custom-call(f32[6,13,4096]{2,1,0:T(8,128)} %x_ref.3), custom_call_target="tpu_custom_call" | custom-call | tf_op jit(solution)/shard_map/pack/pallas_call | solution.py:191
  2.3 7.6 %collective-permute-start.1 = (f32[672,128]{1,0:T(8,128)}, f32[672,128]{1,0:T(8,128)S(1)}, u32[]{:S(2)}, u32[]{:S(2)}) collective-permute-start(f32[672,128]{1,0:T(8,128)} %pack.1), channel_id=1, source_target_pairs={{0,127},{1,0},{2,1},{3,2},{4,3},{5,4},{6,5},{7,6},{8,7},{9,8},{10,... | collective-permute-start | bytes 1032200 | tf_op jit(solution)/shard_map/ppermute | solution.py:185
  9.9 0.0 collective-permute-start
  9.9 7.2 %local.1 = (bf16[384,1152]{1,0:T(8,128)(2,1)}, bf16[384,1152]{1,0:T(8,128)(2,1)}, bf16[1152,384]{1,0:T(8,128)(2,1)}, bf16[1152,384]{1,0:T(8,128)(2,1)}, f32[384,...) custom-call(s32[6,13]{1,0:T(8,128)} %pat_ref.3, f32[6,13,4096]{2,1,0:T(8,128)} %x_ref.3), custom_call_target="tpu_custom_call" | custom-call | tf_op jit(solution)/shard_map/local/pallas_call | solution.py:196
  17.0 1.0 %collective-permute-done.1.next_ref = f32[672,128]{1,0:T(8,128)S(1)} collective-permute-done((f32[672,128]{1,0:T(8,128)}, f32[672,128]{1,0:T(8,128)S(1)}, u32[]{:S(2)}, u32[]{:S(2)}) %collective-permute-start.1) | collective-permute-done | bytes 344096 | tf_op jit(solution)/shard_map/ppermute | solution.py:185
  18.1 0.0 copy-start
  18.1 5.8 %collective-permute-done.prev_ref = f32[672,128]{1,0:T(8,128)S(1)} collective-permute-done((f32[672,128]{1,0:T(8,128)}, f32[672,128]{1,0:T(8,128)S(1)}, u32[]{:S(2)}, u32[]{:S(2)}) %collective-permute-start) | collective-permute-done | bytes 344096 | tf_op jit(solution)/shard_map/ppermute | solution.py:185
  23.9 0.0 copy-start.1
  23.9 0.0 copy-done
  23.9 0.7 %copy-done.1 = f32[672,128]{1,0:T(8,128)} copy-done((f32[672,128]{1,0:T(8,128)}, f32[672,128]{1,0:T(8,128)S(1)}, u32[]{:S(2)}) %copy-start.1) | copy-done | bytes 344088
  24.6 7.7 %finish.1 = f32[6,13,4096]{2,1,0:T(8,128)} custom-call(s32[6,13]{1,0:T(8,128)} %pat_ref.3, f32[672,128]{1,0:T(8,128)} %copy-done.1, f32[672,128]{1,0:T(8,128)} %copy-done, bf16[384,1152]{1,0:T(8,128)(2,1)} %get-tuple-element.12.xh_ref, bf16[384,1152]{1,0:T(8,128)(2,1)} %get-tuple-element.13.xl_ref, bf16[1152,384]{1,0:T(8,128)(2,1)} %get-tuple-element.14.th_ref, ...), custom_call_target="tpu_custom_call" | custom-call | tf_op jit(solution)/shard_map/finish/pallas_call | solution.py:216
Async XLA Ops:
  2.3 15.8 %collective-permute-start.1 = (f32[672,128]{1,0:T(8,128)}, f32[672,128]{1,0:T(8,128)S(1)}, u32[]{:S(2)}, u32[]{:S(2)}) collective-permute-start(f32[672,128]{1,0:T(8,128)} %pack.1), channel_id=1, source_target_pairs={{0,127},{1,0},{2,1},{3,2},{4,3},{5,4},{6,5},{7,6},{8,7},{9,8},{10,... | collective-permute-start | bytes 1032200 | tf_op jit(solution)/shard_map/ppermute | solution.py:185
  9.9 14.0 %collective-permute-start = (f32[672,128]{1,0:T(8,128)}, f32[672,128]{1,0:T(8,128)S(1)}, u32[]{:S(2)}, u32[]{:S(2)}) collective-permute-start(f32[672,128]{1,0:T(8,128)} %pack.1), channel_id=1, source_target_pairs={{0,1},{1,2},{2,3},{3,4},{4,5},{5,6},{6,7},{7,8},{8,9},{9,10},{10,1... | collective-permute-start | bytes 1032200 | tf_op jit(solution)/shard_map/ppermute | solution.py:185
  18.1 5.8 %copy-start = (f32[672,128]{1,0:T(8,128)}, f32[672,128]{1,0:T(8,128)S(1)}, u32[]{:S(2)}) copy-start(f32[672,128]{1,0:T(8,128)S(1)} %collective-permute-done.1.next_ref) | copy-start | bytes 1032196
  23.9 0.7 %copy-start.1 = (f32[672,128]{1,0:T(8,128)}, f32[672,128]{1,0:T(8,128)S(1)}, u32[]{:S(2)}) copy-start(f32[672,128]{1,0:T(8,128)S(1)} %collective-permute-done.prev_ref) | copy-start | bytes 1032196
where the time goes:
time: 32.5 us; the launch traced here: 32.3 us
  Pallas kernels  17.2 us (53%)
  starting transfers between devices  7.59 us (23%)
  waiting for transfers between devices  6.83 us (21%)
  local copies, waits for them, and re-layouts  0.74 us (2%)
    pallas_call x1, Pallas kernels, shards(): pl.pallas_call(finish_kernel, name='finish', in_specs=[smem] + [vmem] * 9...  7.73 us
    ppermute x2, starting transfers between devices, from_behind(): lax.ppermute(x, axes, [(i, (i + by) % length) for i in range(length)])  7.59 us
    pallas_call x1, Pallas kernels, shards(): pl.pallas_call(local_kernel, name='local', in_specs=[smem, vmem], out_spe...  7.15 us
    ppermute x2, waiting for transfers between devices, from_behind(): lax.ppermute(x, axes, [(i, (i + by) % length) for i in range(length)])  6.83 us
    pallas_call x1, Pallas kernels, shards(): pl.pallas_call(pack_kernel, out_shape=jax.ShapeDtypeStruct((PACKED, LANES...  2.29 us
    unnamed x4, local copies, waits for them, and re-layouts  0.74 us
  transfers between devices with their start and end apart: 2, of which 2 were waited for; matrix products, arithmetic and copies ran while one was open for 0% of the time, Pallas kernels for 22%

commit v1 on v0

--- a/solution.py
+++ b/solution.py
@@ -15,6 +15,7 @@
 PACKED = 672
 F32 = jnp.float32
 BF16 = jnp.bfloat16
+SMALL = pltpu.CompilerParams(vmem_limit_bytes=24 << 20)
 
 
 def lane_is_low(rows):
@@ -185,27 +186,30 @@
     return lax.ppermute(x, axes, [(i, (i + by) % length) for i in range(length)])
 
 
+def on_chip(x):
+    return pltpu.with_memory_space_constraint(x, pltpu.VMEM)
+
+
 def shards(density, pattern):
     smem = pl.BlockSpec(memory_space=pltpu.SMEM)
     vmem = pl.BlockSpec(memory_space=pltpu.VMEM)
-    packed = pl.pallas_call(
-        pack_kernel, out_shape=jax.ShapeDtypeStruct((PACKED, LANES), F32), name="pack"
-    )(density)
+    packed = pl.pallas_call(pack_kernel, out_specs=vmem, out_shape=pltpu.VMEM((PACKED, LANES), F32), name="pack", compiler_params=SMALL)(density)
     prev = from_behind(packed, 1)
     following = from_behind(packed, -1)
     local = pl.pallas_call(
         local_kernel,
         name="local",
+        compiler_params=SMALL,
         in_specs=[smem, vmem],
         out_specs=[vmem] * 7,
         out_shape=[
-            jax.ShapeDtypeStruct((SUP, 3 * SUP), BF16),
-            jax.ShapeDtypeStruct((SUP, 3 * SUP), BF16),
-            jax.ShapeDtypeStruct((3 * SUP, SUP), BF16),
-            jax.ShapeDtypeStruct((3 * SUP, SUP), BF16),
-            jax.ShapeDtypeStruct((SUP, SUP), F32),
-            jax.ShapeDtypeStruct((2, SUP, SUP), F32),
-            jax.ShapeDtypeStruct((2, SUP, SUP), F32),
+            pltpu.VMEM((SUP, 3 * SUP), BF16),
+            pltpu.VMEM((SUP, 3 * SUP), BF16),
+            pltpu.VMEM((3 * SUP, SUP), BF16),
+            pltpu.VMEM((3 * SUP, SUP), BF16),
+            pltpu.VMEM((SUP, SUP), F32),
+            pltpu.VMEM((2, SUP, SUP), F32),
+            pltpu.VMEM((2, SUP, SUP), F32),
         ],
         scratch_shapes=[
             pltpu.VMEM((3 * TILES, SUP, LANES), F32),
@@ -216,6 +220,7 @@
     return pl.pallas_call(
         finish_kernel,
         name="finish",
+        compiler_params=SMALL,
         in_specs=[smem] + [vmem] * 9,
         out_specs=vmem,
         out_shape=jax.ShapeDtypeStruct((ROWS, SLOTS, BLK * BLK), F32),
@@ -227,7 +232,7 @@
             pltpu.VMEM((SUP, 2 * SUP), BF16),
             pltpu.VMEM((3 * TILES, SUP, LANES), F32),
         ],
-    )(pattern, prev, following, *local)
+    )(pattern, *(on_chip(x) for x in (prev, following, *local)))
 
 
 def solution(mesh):

time: 32.5 us -> 28.5 us (0.88)
  Pallas kernels: 17.2 us -> 10.9 us
  waiting for transfers between devices: 6.83 us -> 8.31 us
  local copies, waits for them, and re-layouts: 0.74 us -> 1.41 us
    pallas_call x3, Pallas kernels: 17.2 us -> 10.9 us  [the longest x1 5.45 us: shards(): pl.pallas_call(local_kernel, name='local', compiler_params=SMALL, in_spec...]
    ppermute x2, waiting for transfers between devices: 6.83 us -> 8.31 us  [from_behind(): lax.ppermute(x, axes, [(i, (i + by) % length) for i in range(length)])]
    unnamed x4, local copies, waits for them, and re-layouts: 0.74 us -> 1.41 us
  transfers between devices with their start and end apart: 2 -> 2, of which waited for: 2 -> 2; matrix products, arithmetic and copies ran while one was open for 0% -> 0% of each run, Pallas kernels for 22% -> 19%
where the time goes in v1:
time: 28.5 us; the launch traced here: 28.3 us
  Pallas kernels  10.9 us (38%)
  waiting for transfers between devices  8.31 us (29%)
  starting transfers between devices  7.66 us (27%)
  local copies, waits for them, and re-layouts  1.41 us (5%)
    ppermute x2, waiting for transfers between devices, from_behind(): lax.ppermute(x, axes, [(i, (i + by) % length) for i in range(length)])  8.31 us
    ppermute x2, starting transfers between devices, from_behind(): lax.ppermute(x, axes, [(i, (i + by) % length) for i in range(length)])  7.66 us
    pallas_call x1, Pallas kernels, shards(): pl.pallas_call(local_kernel, name='local', compiler_params=SMALL, in_spec...  5.45 us
    pallas_call x1, Pallas kernels, shards(): pl.pallas_call(finish_kernel, name='finish', compiler_params=SMALL, in_sp...  5.34 us
    unnamed x4, local copies, waits for them, and re-layouts  1.41 us
  transfers between devices with their start and end apart: 2, of which 2 were waited for; matrix products, arithmetic and copies ran while one was open for 0% of the time, Pallas kernels for 19%

profile of v1, /device:TPU:1, one launch (start us, length us, event | category | flops | bytes accessed | tf_op | source)
XLA Modules:
  0.0 28.3 jit_solution(912453121987540819)
XLA Ops:
  0.0 0.0 copy-start
  0.0 1.4 %copy-done = f32[6,13,4096]{2,1,0:T(8,128)S(1)} copy-done((f32[6,13,4096]{2,1,0:T(8,128)S(1)}, f32[6,13,4096]{2,1,0:T(8,128)}, u32[]{:S(2)}) %copy-start) | copy-done | bytes 1277976
  1.4 0.0 copy-start.1
  1.4 0.1 pack.1
  1.6 7.7 %collective-permute-start.1 = (f32[672,128]{1,0:T(8,128)S(1)}, f32[672,128]{1,0:T(8,128)S(1)}, u32[]{:S(2)}, u32[]{:S(2)}) collective-permute-start(f32[672,128]{1,0:T(8,128)S(1)} %pack.1), channel_id=1, source_target_pairs={{0,127},{1,0},{2,1},{3,2},{4,3},{5,4},{6,5},{7,6},{8,7},{9,8},{10,... | collective-permute-start | bytes 1032200 | tf_op jit(solution)/shard_map/ppermute | solution.py:186
  9.2 0.0 collective-permute-start
  9.2 0.0 copy-done.1
  9.2 5.5 %local.1 = (bf16[384,1152]{1,0:T(8,128)(2,1)S(1)}, bf16[384,1152]{1,0:T(8,128)(2,1)S(1)}, bf16[1152,384]{1,0:T(8,128)(2,1)S(1)}, bf16[1152,384]{1,0:T(8,128)(2,1...) custom-call(s32[6,13]{1,0:T(8,128)S(1)} %copy-done.1, ...), custom_call_target="tpu_custom_call" | custom-call | tf_op jit(solution)/shard_map/local/pallas_call | solution.py:199
  14.7 2.4 %collective-permute-done.1.next_ref = f32[672,128]{1,0:T(8,128)S(1)} collective-permute-done((f32[672,128]{1,0:T(8,128)S(1)}, f32[672,128]{1,0:T(8,128)S(1)}, u32[]{:S(2)}, u32[]{:S(2)}) %collective-permute-start.1) | collective-permute-done | bytes 344096 | tf_op jit(solution)/shard_map/ppermute | solution.py:186
  17.1 5.9 %collective-permute-done.prev_ref = f32[672,128]{1,0:T(8,128)S(1)} collective-permute-done((f32[672,128]{1,0:T(8,128)S(1)}, f32[672,128]{1,0:T(8,128)S(1)}, u32[]{:S(2)}, u32[]{:S(2)}) %collective-permute-start) | collective-permute-done | bytes 344096 | tf_op jit(solution)/shard_map/ppermute | solution.py:186
  23.0 5.3 %finish.1 = f32[6,13,4096]{2,1,0:T(8,128)} custom-call(s32[6,13]{1,0:T(8,128)S(1)} %copy-done.1, f32[672,128]{1,0:T(8,128)S(1)} %collective-permute-done.prev_ref, f32[672,128]{1,0:T(8,128)S(1)} %collective-permute-done.1.next_ref, bf16[384,1152]{1,0:T(8,128)(2,1)S(1)} %get-tuple-element.12.xh_ref, bf16[384,1152]{1,0:T(8,128)(2,1)S(1)} %get-tuple-element.13.xl_ref, ...), custom_call_target="tpu_custom_call" | custom-call | tf_op jit(solution)/shard_map/finish/pallas_call | solution.py:220
Async XLA Ops:
  0.0 1.4 %copy-start = (f32[6,13,4096]{2,1,0:T(8,128)S(1)}, f32[6,13,4096]{2,1,0:T(8,128)}, u32[]{:S(2)}) copy-start(f32[6,13,4096]{2,1,0:T(8,128)} %x_ref.3) | copy-start | bytes 3833860
  1.4 7.8 %copy-start.1 = (s32[6,13]{1,0:T(8,128)S(1)}, s32[6,13]{1,0:T(8,128)}, u32[]{:S(2)}) copy-start(s32[6,13]{1,0:T(8,128)} %pat_ref.3) | copy-start | bytes 940
  1.6 15.5 %collective-permute-start.1 = (f32[672,128]{1,0:T(8,128)S(1)}, f32[672,128]{1,0:T(8,128)S(1)}, u32[]{:S(2)}, u32[]{:S(2)}) collective-permute-start(f32[672,128]{1,0:T(8,128)S(1)} %pack.1), channel_id=1, source_target_pairs={{0,127},{1,0},{2,1},{3,2},{4,3},{5,4},{6,5},{7,6},{8,7},{9,8},{10,... | collective-permute-start | bytes 1032200 | tf_op jit(solution)/shard_map/ppermute | solution.py:186
  9.2 13.8 %collective-permute-start = (f32[672,128]{1,0:T(8,128)S(1)}, f32[672,128]{1,0:T(8,128)S(1)}, u32[]{:S(2)}, u32[]{:S(2)}) collective-permute-start(f32[672,128]{1,0:T(8,128)S(1)} %pack.1), channel_id=1, source_target_pairs={{0,1},{1,2},{2,3},{3,4},{4,5},{5,6},{6,7},{7,8},{8,9},{9,10},{10,1... | collective-permute-start | bytes 1032200 | tf_op jit(solution)/shard_map/ppermute | solution.py:186

commit v2 on v1

--- a/solution.py
+++ b/solution.py
@@ -62,7 +62,12 @@
     return jnp.where(lane_is_low(8), values[0], values[1])[:1]
 
 
-def pack_kernel(x_ref, out_ref):
+def pack_kernel(hbm_ref, out_ref, x_ref, sems):
+    copies = [pltpu.make_async_copy(hbm_ref.at[row], x_ref.at[row], sems.at[row]) for row in range(ROWS)]
+    for copy in copies:
+        copy.start()
+    for copy in copies:
+        copy.wait()
     first = 0
     for p in range(TILES):
         for row in (2 * p, 2 * p + 1):
@@ -193,9 +198,18 @@
 def shards(density, pattern):
     smem = pl.BlockSpec(memory_space=pltpu.SMEM)
     vmem = pl.BlockSpec(memory_space=pltpu.VMEM)
-    packed = pl.pallas_call(pack_kernel, out_specs=vmem, out_shape=pltpu.VMEM((PACKED, LANES), F32), name="pack", compiler_params=SMALL)(density)
+    packed, density = pl.pallas_call(
+        pack_kernel,
+        name="pack",
+        compiler_params=SMALL,
+        in_specs=[pl.BlockSpec(memory_space=pltpu.HBM)],
+        out_specs=[vmem] * 2,
+        out_shape=[pltpu.VMEM((PACKED, LANES), F32), pltpu.VMEM((ROWS, SLOTS, BLK * BLK), F32)],
+        scratch_shapes=[pltpu.SemaphoreType.DMA((ROWS,))],
+    )(pltpu.with_memory_space_constraint(density, pltpu.HBM))
+    density = on_chip(density)
+    following = from_behind(packed, -1)
     prev = from_behind(packed, 1)
-    following = from_behind(packed, -1)
     local = pl.pallas_call(
         local_kernel,
         name="local",

time: 28.5 us -> 23.3 us (0.82)
  waiting for transfers between devices: 8.31 us -> 3.07 us
  Pallas kernels: 10.9 us -> 12.4 us
  local copies, waits for them, and re-layouts: 1.41 us -> 0.01 us
    ppermute x2, waiting for transfers between devices: 8.31 us -> 3.07 us  [from_behind(): lax.ppermute(x, axes, [(i, (i + by) % length) for i in range(length)])]
    pallas_call x1, Pallas kernels: 0.15 us -> 1.56 us  [shards(): pl.pallas_call(pack_kernel, name='pack', compiler_params=SMALL, in_specs=...]
    unnamed x4 -> x2, local copies, waits for them, and re-layouts: 1.41 us -> 0.01 us
  transfers between devices with their start and end apart: 2 -> 2, of which waited for: 2 -> 1; matrix products, arithmetic and copies ran while one was open for 0% -> 0% of each run, Pallas kernels for 19% -> 24%
where the time goes in v2:
time: 23.3 us; the launch traced here: 23.2 us
  Pallas kernels  12.4 us (53%)
  starting transfers between devices  7.74 us (33%)
  waiting for transfers between devices  3.07 us (13%)
    ppermute x2, starting transfers between devices, from_behind(): lax.ppermute(x, axes, [(i, (i + by) % length) for i in range(length)])  7.74 us
    pallas_call x1, Pallas kernels, shards(): pl.pallas_call(local_kernel, name='local', compiler_params=SMALL, in_spec...  5.45 us
    pallas_call x1, Pallas kernels, shards(): pl.pallas_call(finish_kernel, name='finish', compiler_params=SMALL, in_sp...  5.34 us
    ppermute x2, waiting for transfers between devices, from_behind(): lax.ppermute(x, axes, [(i, (i + by) % length) for i in range(length)])  3.07 us
    pallas_call x1, Pallas kernels, shards(): pl.pallas_call(pack_kernel, name='pack', compiler_params=SMALL, in_specs=...  1.56 us
  transfers between devices with their start and end apart: 2, of which 1 were waited for; matrix products, arithmetic and copies ran while one was open for 0% of the time, Pallas kernels for 24%

profile of v2, /device:TPU:1, one launch (start us, length us, event | category | flops | bytes accessed | tf_op | source)
XLA Modules:
  0.0 23.2 jit_solution(4673656435415305484)
XLA Ops:
  0.0 0.0 copy-start
  0.0 1.6 %pack.1 = (f32[672,128]{1,0:T(8,128)S(1)}, f32[6,13,4096]{2,1,0:T(8,128)S(1)}) custom-call(f32[6,13,4096]{2,1,0:T(8,128)} %hbm_ref.1), custom_call_target="tpu_custom_call" | custom-call | tf_op jit(solution)/shard_map/pack/pallas_call | solution.py:201
  1.6 2.5 %collective-permute-start = (f32[672,128]{1,0:T(8,128)S(1)}, f32[672,128]{1,0:T(8,128)S(1)}, u32[]{:S(2)}, u32[]{:S(2)}) collective-permute-start(f32[672,128]{1,0:T(8,128)S(1)} %get-tuple-element.14), channel_id=1, source_target_pairs={{0,1},{1,2},{2,3},{3,4},{4,5},{5,6},{6,7},{7,8},{8,9},{9,10},{10,1... | collective-permute-start | bytes 1032200 | tf_op jit(solution)/shard_map/ppermute | solution.py:191
  4.1 5.2 %collective-permute-start.1 = (f32[672,128]{1,0:T(8,128)S(1)}, f32[672,128]{1,0:T(8,128)S(1)}, u32[]{:S(2)}, u32[]{:S(2)}) collective-permute-start(f32[672,128]{1,0:T(8,128)S(1)} %get-tuple-element.14), channel_id=1, source_target_pairs={{0,127},{1,0},{2,1},{3,2},{4,3},{5,4},{6,5},{7,6},{8,7},{9,8},{10,... | collective-permute-start | bytes 1032200 | tf_op jit(solution)/shard_map/ppermute | solution.py:191
  9.3 0.0 copy-done
  9.3 5.5 %local.1 = (bf16[384,1152]{1,0:T(8,128)(2,1)S(1)}, bf16[384,1152]{1,0:T(8,128)(2,1)S(1)}, bf16[1152,384]{1,0:T(8,128)(2,1)S(1)}, bf16[1152,384]{1,0:T(8,128)(2,1...) custom-call(s32[6,13]{1,0:T(8,128)S(1)} %copy-done, ...), custom_call_target="tpu_custom_call" | custom-call | tf_op jit(solution)/shard_map/local/pallas_call | solution.py:213
  14.8 3.1 %collective-permute-done.prev_ref = f32[672,128]{1,0:T(8,128)S(1)} collective-permute-done((f32[672,128]{1,0:T(8,128)S(1)}, f32[672,128]{1,0:T(8,128)S(1)}, u32[]{:S(2)}, u32[]{:S(2)}) %collective-permute-start) | collective-permute-done | bytes 344096 | tf_op jit(solution)/shard_map/ppermute | solution.py:191
  17.9 0.0 collective-permute-done.1.next_ref
  17.9 5.3 %finish.1 = f32[6,13,4096]{2,1,0:T(8,128)} custom-call(s32[6,13]{1,0:T(8,128)S(1)} %copy-done, f32[672,128]{1,0:T(8,128)S(1)} %collective-permute-done.prev_ref, f32[672,128]{1,0:T(8,128)S(1)} %collective-permute-done.1.next_ref, bf16[384,1152]{1,0:T(8,128)(2,1)S(1)} %get-tuple-element.16.xh_ref, bf16[384,1152]{1,0:T(8,128)(2,1)S(1)} %get-tuple-element.17.xl_ref, ...), custom_call_target="tpu_custom_call" | custom-call | tf_op jit(solution)/shard_map/finish/pallas_call | solution.py:234
Async XLA Ops:
  0.0 9.3 %copy-start = (s32[6,13]{1,0:T(8,128)S(1)}, s32[6,13]{1,0:T(8,128)}, u32[]{:S(2)}) copy-start(s32[6,13]{1,0:T(8,128)} %pat_ref.3) | copy-start | bytes 940
  1.6 16.3 %collective-permute-start = (f32[672,128]{1,0:T(8,128)S(1)}, f32[672,128]{1,0:T(8,128)S(1)}, u32[]{:S(2)}, u32[]{:S(2)}) collective-permute-start(f32[672,128]{1,0:T(8,128)S(1)} %get-tuple-element.14), channel_id=1, source_target_pairs={{0,1},{1,2},{2,3},{3,4},{4,5},{5,6},{6,7},{7,8},{8,9},{9,10},{10,1... | collective-permute-start | bytes 1032200 | tf_op jit(solution)/shard_map/ppermute | solution.py:191
  4.1 13.8 %collective-permute-start.1 = (f32[672,128]{1,0:T(8,128)S(1)}, f32[672,128]{1,0:T(8,128)S(1)}, u32[]{:S(2)}, u32[]{:S(2)}) collective-permute-start(f32[672,128]{1,0:T(8,128)S(1)} %get-tuple-element.14), channel_id=1, source_target_pairs={{0,127},{1,0},{2,1},{3,2},{4,3},{5,4},{6,5},{7,6},{8,7},{9,8},{10,... | collective-permute-start | bytes 1032200 | tf_op jit(solution)/shard_map/ppermute | solution.py:191

commit v3 on v2

--- a/solution.py
+++ b/solution.py
@@ -12,7 +12,6 @@
 SUP = ROWS * BLK
 LANES = 128
 TILES = SUP // LANES
-PACKED = 672
 F32 = jnp.float32
 BF16 = jnp.bfloat16
 SMALL = pltpu.CompilerParams(vmem_limit_bytes=24 << 20)
@@ -62,60 +61,66 @@
     return jnp.where(lane_is_low(8), values[0], values[1])[:1]
 
 
+def packed_rows():
+    first = {}
+    for p in range(TILES):
+        for row in (2 * p, 2 * p + 1):
+            for q in range(p + row % 2, TILES):
+                first[row, q] = BLK * len(first)
+    return first
+
+
+FIRST = packed_rows()
+DIAGONALS = BLK * len(FIRST)
+PACKED = DIAGONALS + 8
+
+
 def pack_kernel(hbm_ref, out_ref, x_ref, sems):
     copies = [pltpu.make_async_copy(hbm_ref.at[row], x_ref.at[row], sems.at[row]) for row in range(ROWS)]
     for copy in copies:
         copy.start()
     for copy in copies:
         copy.wait()
-    first = 0
-    for p in range(TILES):
-        for row in (2 * p, 2 * p + 1):
-            for q in range(p, TILES):
-                if q == p and row % 2:
-                    continue
-                slot = 2 * q - row + HALF
-                store_pair(out_ref, (), first, load_block(x_ref, row, slot), load_block(x_ref, row, slot + 1))
-                first += BLK
-    store_pair(out_ref, (), first, load_block(x_ref, 1, HALF), load_block(x_ref, 3, HALF))
-    first += BLK
-    out_ref[first : first + BLK // 2, :] = load_block(x_ref, 5, HALF)
-
-
-def unpack(rec_ref, tri_ref):
-    first = 0
-    zeros = jnp.zeros((BLK, LANES), F32)
-    for p in range(TILES):
-        for row in (2 * p, 2 * p + 1):
-            for q in range(p, TILES):
-                if q == p and row % 2:
-                    continue
-                tri_ref[q, row * BLK : (row + 1) * BLK, :] = rec_ref[first : first + BLK, :]
-                first += BLK
-    corner = rec_ref[first : first + BLK, :]
-    low = lane_is_low(BLK)
-    tri_ref[0, BLK : 2 * BLK, :] = jnp.where(low, zeros, pltpu.roll(corner, BLK, 1))
-    tri_ref[1, 3 * BLK : 4 * BLK, :] = jnp.where(low, zeros, corner)
-    first += BLK
-    last = rec_ref[first : first + BLK // 2, :]
-    store_pair(tri_ref, (2,), 5 * BLK, jnp.zeros((BLK // 2, LANES), F32), last)
-
-
-def unpack_split(rec_ref, tri_ref, hi_ref, lo_ref):
-    unpack(rec_ref, tri_ref)
-    shape = (LANES, LANES)
-    corner = (lax.broadcasted_iota(jnp.int32, shape, 0) >= BLK) & (lax.broadcasted_iota(jnp.int32, shape, 1) < BLK)
+    half = BLK // 2
+    lane = lax.broadcasted_iota(jnp.int32, (half, LANES), 1)
+    even_row = 2 * lax.broadcasted_iota(jnp.int32, (half, LANES), 0)
+    for (row, q), first in FIRST.items():
+        slot = 2 * q - row + HALF
+        even, odd = even_odd_rows(load_block(x_ref, row, slot), load_block(x_ref, row, slot + 1))
+        if q == row // 2:
+            lent_even = load_block(x_ref, row + 1, HALF)
+            lent_odd = pltpu.roll(lent_even, BLK, 1)
+            low = lane < BLK
+            even = jnp.where(low & (even_row > lane), lent_even, even)
+            odd = jnp.where(low & (even_row + 1 > lane), lent_odd, odd)
+            diagonal = jnp.where(even_row == lane, lent_even, 0.0) + jnp.where(even_row + 1 == lane, lent_odd, 0.0)
+            out_ref[DIAGONALS + q : DIAGONALS + q + 1, :] = jnp.sum(diagonal, 0, keepdims=True)
+        out_ref[pl.ds(first, half, stride=2), :] = even
+        out_ref[pl.ds(first + 1, half, stride=2), :] = odd
+    out_ref[DIAGONALS + TILES :, :] = jnp.zeros((8 - TILES, LANES), F32)
+
+
+def unpack_split(rec_ref, hi_ref, lo_ref):
+    lane = lax.broadcasted_iota(jnp.int32, (BLK, LANES), 1)
+    line = lax.broadcasted_iota(jnp.int32, (BLK, LANES), 0)
+    low = lane < BLK
     for p in range(TILES):
         for q in range(p, TILES):
-            tile = tri_ref[q, p * LANES : (p + 1) * LANES, :]
-            turned = tile.T
             here = (slice(p * LANES, (p + 1) * LANES), slice(q * LANES, (q + 1) * LANES))
             there = (here[1], here[0])
+            top = rec_ref[FIRST[2 * p, q] : FIRST[2 * p, q] + BLK, :]
             if p == q:
-                hi_ref[here], lo_ref[here] = split(jnp.where(corner, turned, tile))
+                turned = jnp.concatenate([top, top], 0).T
+                upper = jnp.where(low & (line > lane), turned[:BLK], top)
+                diagonal = jnp.broadcast_to(rec_ref[DIAGONALS + q : DIAGONALS + q + 1, :], (BLK, LANES))
+                lent = jnp.where(line > lane, top, jnp.where(line < lane, turned[:BLK], diagonal))
+                lower = jnp.where(low, turned[BLK:], pltpu.roll(lent, BLK, 1))
+                hi_ref[here], lo_ref[here] = split(jnp.concatenate([upper, lower], 0))
             else:
+                bottom = rec_ref[FIRST[2 * p + 1, q] : FIRST[2 * p + 1, q] + BLK, :]
+                tile = jnp.concatenate([top, bottom], 0)
                 hi_ref[here], lo_ref[here] = split(tile)
-                hi_ref[there], lo_ref[there] = split(turned)
+                hi_ref[there], lo_ref[there] = split(tile.T)
 
 
 def local_kernel(pat_ref, x_ref, xh_ref, xl_ref, th_ref, tl_ref, base_ref, part_ref, side_ref, nat_ref, sqh_ref, sql_ref):
@@ -144,36 +149,93 @@
     base_ref[...] = 3.0 * base_ref[...] - 2.0 * cube
 
 
+def corner_product(side, ah, al, bh, bl):
+    wide, narrow = ((0, 2), (2, 3)) if side else ((1, 3), (0, 1))
+    (w0, w1), (n0, n1) = (tuple(LANES * t for t in span) for span in (wide, narrow))
+    w, n = slice(w0, w1), slice(n0, n1)
+    main = dot3(ah[:, w], al[:, w], bh[w, w], bl[w, w])
+    extra = dot3(ah[n, n], al[n, n], bh[n, w], bl[n, w])
+    own = dot3(ah[n, :], al[n, :], bh[:, n], bl[:, n])
+    return main, extra, own
+
+
+def corner_tile(side, parts, p, t):
+    main, extra, own = parts
+    if (t > p) if side else (t < p):
+        return None
+    far = TILES - 1 if side else 0
+    rows = slice(p * LANES, (p + 1) * LANES)
+    if t == far:
+        return own
+    base = 0 if side else 1
+    lanes = slice((t - base) * LANES, (t - base + 1) * LANES)
+    if p == far:
+        return main[rows, lanes] + extra[:, lanes]
+    return main[rows, lanes]
+
+
 def finish_kernel(
     pat_ref, prev_ref, next_ref, xh_ref, xl_ref, th_ref, tl_ref, base_ref, part_ref, side_ref,
-    out_ref, tri_ref, dh_ref, dl_ref, eh_ref, el_ref, nat_ref,
+    out_hbm, dh_ref, dl_ref, eh_ref, el_ref, nat_ref, out_ref, sems,
 ):
     for side, rec_ref in ((0, prev_ref), (1, next_ref)):
-        unpack_split(rec_ref, tri_ref.at[side], dh_ref.at[side], dl_ref.at[side])
+        unpack_split(rec_ref, dh_ref.at[side], dl_ref.at[side])
     for side in (0, 1):
         cols = slice(2 * side * SUP, (2 * side + 1) * SUP)
-        edge = part_ref[side] + dot3(xh_ref[:, cols], xl_ref[:, cols], dh_ref[side], dl_ref[side])
-        for row in range(ROWS):
-            rows = slice(row * BLK, (row + 1) * BLK)
+        parts = corner_product(side, xh_ref[:, cols], xl_ref[:, cols], dh_ref[side], dl_ref[side])
+        for p in range(TILES):
             for t in range(TILES):
+                edge = corner_tile(side, parts, p, t)
+                lanes = slice(side * SUP + t * LANES, side * SUP + (t + 1) * LANES)
                 tile = 2 * side * TILES + t
-                lanes = slice(t * LANES, (t + 1) * LANES)
-                kept = edge[rows, lanes] * mask_tile(pat_ref, row, tile)
-                nat_ref[tile, rows, :] = 3.0 * kept
-                lanes = slice(side * SUP + t * LANES, side * SUP + (t + 1) * LANES)
-                eh_ref[rows, lanes], el_ref[rows, lanes] = split(kept)
+                if edge is None:
+                    nothing = jnp.zeros((LANES, LANES), BF16)
+                    eh_ref[p * LANES : (p + 1) * LANES, lanes] = nothing
+                    el_ref[p * LANES : (p + 1) * LANES, lanes] = nothing
+                    continue
+                edge = edge + part_ref[side, p * LANES : (p + 1) * LANES, t * LANES : (t + 1) * LANES]
+                for row in (2 * p, 2 * p + 1):
+                    rows = slice(row * BLK, (row + 1) * BLK)
+                    kept = edge[row % 2 * BLK : (row % 2 + 1) * BLK] * mask_tile(pat_ref, row, tile)
+                    nat_ref[tile, rows, :] = 3.0 * kept
+                    eh_ref[rows, lanes], el_ref[rows, lanes] = split(kept)
+    wide0, narrow0 = slice(LANES, SUP), slice(0, LANES)
+    wide1, narrow1 = slice(0, 2 * LANES), slice(2 * LANES, SUP)
+    eh, el = (ref[:, :SUP] for ref in (eh_ref, el_ref))
+    fh, fl = (ref[:, SUP:] for ref in (eh_ref, el_ref))
+    lh, ll = (ref[:SUP, :] for ref in (th_ref, tl_ref))
+    uh, ul = (ref[2 * SUP :, :] for ref in (th_ref, tl_ref))
+    main = dot3(
+        jnp.concatenate([eh[:, wide0], fh[:, wide1]], 1),
+        jnp.concatenate([el[:, wide0], fl[:, wide1]], 1),
+        jnp.concatenate([lh[wide0, :], uh[wide1, :]], 0),
+        jnp.concatenate([ll[wide0, :], ul[wide1, :]], 0),
+    )
+    first = dot3(eh[narrow0, narrow0], el[narrow0, narrow0], lh[narrow0, narrow0], ll[narrow0, narrow0])
+    last = dot3(fh[narrow1, narrow1], fl[narrow1, narrow1], uh[narrow1, narrow1], ul[narrow1, narrow1])
+    for p in range(TILES):
+        rows = slice(p * LANES, (p + 1) * LANES)
+        for t in range(TILES):
+            lanes = slice(t * LANES, (t + 1) * LANES)
+            cube = main[rows, lanes]
+            if p == t == 0:
+                cube = cube + first
+            if p == t == TILES - 1:
+                cube = cube + last
+            nat_ref[TILES + t, rows, :] = base_ref[rows, lanes] - 2.0 * cube
     for side in (0, 1):
         cols = slice(side * SUP, (side + 1) * SUP)
-        cube = side_ref[side] + dot3(eh_ref[:, cols], el_ref[:, cols], dh_ref[side], dl_ref[side])
-        for t in range(TILES):
-            tile = 2 * side * TILES + t
-            nat_ref[tile] = nat_ref[tile] - 2.0 * cube[:, t * LANES : (t + 1) * LANES]
-    turned_h = jnp.concatenate([th_ref[:SUP, :], th_ref[2 * SUP :, :]], 0)
-    turned_l = jnp.concatenate([tl_ref[:SUP, :], tl_ref[2 * SUP :, :]], 0)
-    cube = dot3(eh_ref[...], el_ref[...], turned_h, turned_l)
-    for t in range(TILES):
-        lanes = slice(t * LANES, (t + 1) * LANES)
-        nat_ref[TILES + t] = base_ref[:, lanes] - 2.0 * cube[:, lanes]
+        parts = corner_product(side, eh_ref[:, cols], el_ref[:, cols], dh_ref[side], dl_ref[side])
+        for p in range(TILES):
+            rows = slice(p * LANES, (p + 1) * LANES)
+            for t in range(TILES):
+                cube = corner_tile(side, parts, p, t)
+                if cube is None:
+                    continue
+                tile = 2 * side * TILES + t
+                cube = cube + side_ref[side, rows, t * LANES : (t + 1) * LANES]
+                nat_ref[tile, rows, :] = nat_ref[tile, rows, :] - 2.0 * cube
+    copies = []
     for row in range(ROWS):
         for tile in range(row // 2, (row + SLOTS - 1) // 2 + 1):
             mask = mask_tile(pat_ref, row, tile)
@@ -183,6 +245,10 @@
             for slot, block in ((2 * tile - row, left), (2 * tile + 1 - row, right)):
                 if 0 <= slot < SLOTS:
                     out_ref[row, slot, :] = block.reshape(BLK * BLK)
+        copies.append(pltpu.make_async_copy(out_ref.at[row], out_hbm.at[row], sems.at[row]))
+        copies[-1].start()
+    for copy in copies:
+        copy.wait()
 
 
 def from_behind(x, by):
@@ -236,15 +302,16 @@
         name="finish",
         compiler_params=SMALL,
         in_specs=[smem] + [vmem] * 9,
-        out_specs=vmem,
+        out_specs=pl.BlockSpec(memory_space=pltpu.HBM),
         out_shape=jax.ShapeDtypeStruct((ROWS, SLOTS, BLK * BLK), F32),
         scratch_shapes=[
-            pltpu.VMEM((2, TILES, SUP, LANES), F32),
             pltpu.VMEM((2, SUP, SUP), BF16),
             pltpu.VMEM((2, SUP, SUP), BF16),
             pltpu.VMEM((SUP, 2 * SUP), BF16),
             pltpu.VMEM((SUP, 2 * SUP), BF16),
             pltpu.VMEM((3 * TILES, SUP, LANES), F32),
+            pltpu.VMEM((ROWS, SLOTS, BLK * BLK), F32),
+            pltpu.SemaphoreType.DMA((ROWS,)),
         ],
     )(pattern, *(on_chip(x) for x in (prev, following, *local)))
 

time: 23.3 us -> 21.1 us (0.906)
  Pallas kernels: 12.4 us -> 11.1 us
  waiting for transfers between devices: 3.07 us -> 2.1 us
    pallas_call x1, Pallas kernels: 5.34 us -> 4.08 us  [shards(): pl.pallas_call(finish_kernel, name='finish', compiler_params=SMALL, in_sp...]
    ppermute x2, waiting for transfers between devices: 3.07 us -> 2.1 us  [from_behind(): lax.ppermute(x, axes, [(i, (i + by) % length) for i in range(length)])]
  transfers between devices with their start and end apart: 2 -> 2, of which waited for: 1 -> 1; matrix products, arithmetic and copies ran while one was open for 0% -> 0% of each run, Pallas kernels for 24% -> 26%
where the time goes in v3:
time: 21.1 us; the launch traced here: 21 us
  Pallas kernels  11.1 us (53%)
  starting transfers between devices  7.74 us (37%)
  waiting for transfers between devices  2.1 us (10%)
    ppermute x2, starting transfers between devices, from_behind(): lax.ppermute(x, axes, [(i, (i + by) % length) for i in range(length)])  7.74 us
    pallas_call x1, Pallas kernels, shards(): pl.pallas_call(local_kernel, name='local', compiler_params=SMALL, in_spec...  5.47 us
    pallas_call x1, Pallas kernels, shards(): pl.pallas_call(finish_kernel, name='finish', compiler_params=SMALL, in_sp...  4.08 us
    ppermute x2, waiting for transfers between devices, from_behind(): lax.ppermute(x, axes, [(i, (i + by) % length) for i in range(length)])  2.1 us
    pallas_call x1, Pallas kernels, shards(): pl.pallas_call(pack_kernel, name='pack', compiler_params=SMALL, in_specs=...  1.57 us
  transfers between devices with their start and end apart: 2, of which 1 were waited for; matrix products, arithmetic and copies ran while one was open for 0% of the time, Pallas kernels for 26%

profile of v3, /device:TPU:1, one launch (start us, length us, event | category | flops | bytes accessed | tf_op | source)
XLA Modules:
  0.0 21.0 jit_solution(17426257685233224268)
XLA Ops:
  0.0 0.0 copy-start
  0.0 1.6 %pack.1 = (f32[584,128]{1,0:T(8,128)S(1)}, f32[6,13,4096]{2,1,0:T(8,128)S(1)}) custom-call(f32[6,13,4096]{2,1,0:T(8,128)} %hbm_ref.1), custom_call_target="tpu_custom_call" | custom-call | tf_op jit(solution)/shard_map/pack/pallas_call | solution.py:267
  1.6 2.5 %collective-permute-start = (f32[584,128]{1,0:T(8,128)S(1)}, f32[584,128]{1,0:T(8,128)S(1)}, u32[]{:S(2)}, u32[]{:S(2)}) collective-permute-start(f32[584,128]{1,0:T(8,128)S(1)} %get-tuple-element.14), channel_id=1, source_target_pairs={{0,1},{1,2},{2,3},{3,4},{4,5},{5,6},{6,7},{7,8},{8,9},{9,10},{10,1... | collective-permute-start | bytes 897032 | tf_op jit(solution)/shard_map/ppermute | solution.py:257
  4.1 5.2 %collective-permute-start.1 = (f32[584,128]{1,0:T(8,128)S(1)}, f32[584,128]{1,0:T(8,128)S(1)}, u32[]{:S(2)}, u32[]{:S(2)}) collective-permute-start(f32[584,128]{1,0:T(8,128)S(1)} %get-tuple-element.14), channel_id=1, source_target_pairs={{0,127},{1,0},{2,1},{3,2},{4,3},{5,4},{6,5},{7,6},{8,7},{9,8},{10,... | collective-permute-start | bytes 897032 | tf_op jit(solution)/shard_map/ppermute | solution.py:257
  9.3 0.0 copy-done
  9.3 5.5 %local.1 = (bf16[384,1152]{1,0:T(8,128)(2,1)S(1)}, bf16[384,1152]{1,0:T(8,128)(2,1)S(1)}, bf16[1152,384]{1,0:T(8,128)(2,1)S(1)}, bf16[1152,384]{1,0:T(8,128)(2,1...) custom-call(s32[6,13]{1,0:T(8,128)S(1)} %copy-done, ...), custom_call_target="tpu_custom_call" | custom-call | tf_op jit(solution)/shard_map/local/pallas_call | solution.py:279
  14.8 2.1 %collective-permute-done.prev_ref = f32[584,128]{1,0:T(8,128)S(1)} collective-permute-done((f32[584,128]{1,0:T(8,128)S(1)}, f32[584,128]{1,0:T(8,128)S(1)}, u32[]{:S(2)}, u32[]{:S(2)}) %collective-permute-start) | collective-permute-done | bytes 299040 | tf_op jit(solution)/shard_map/ppermute | solution.py:257
  16.9 0.0 collective-permute-done.1.next_ref
  16.9 4.1 %finish.1 = f32[6,13,4096]{2,1,0:T(8,128)} custom-call(s32[6,13]{1,0:T(8,128)S(1)} %copy-done, f32[584,128]{1,0:T(8,128)S(1)} %collective-permute-done.prev_ref, f32[584,128]{1,0:T(8,128)S(1)} %collective-permute-done.1.next_ref, bf16[384,1152]{1,0:T(8,128)(2,1)S(1)} %get-tuple-element.16.xh_ref, bf16[384,1152]{1,0:T(8,128)(2,1)S(1)} %get-tuple-element.17.xl_ref, ...), custom_call_target="tpu_custom_call" | custom-call | tf_op jit(solution)/shard_map/finish/pallas_call | solution.py:300
Async XLA Ops:
  0.0 9.3 %copy-start = (s32[6,13]{1,0:T(8,128)S(1)}, s32[6,13]{1,0:T(8,128)}, u32[]{:S(2)}) copy-start(s32[6,13]{1,0:T(8,128)} %pat_ref.3) | copy-start | bytes 940
  1.6 15.3 %collective-permute-start = (f32[584,128]{1,0:T(8,128)S(1)}, f32[584,128]{1,0:T(8,128)S(1)}, u32[]{:S(2)}, u32[]{:S(2)}) collective-permute-start(f32[584,128]{1,0:T(8,128)S(1)} %get-tuple-element.14), channel_id=1, source_target_pairs={{0,1},{1,2},{2,3},{3,4},{4,5},{5,6},{6,7},{7,8},{8,9},{9,10},{10,1... | collective-permute-start | bytes 897032 | tf_op jit(solution)/shard_map/ppermute | solution.py:257
  4.1 12.8 %collective-permute-start.1 = (f32[584,128]{1,0:T(8,128)S(1)}, f32[584,128]{1,0:T(8,128)S(1)}, u32[]{:S(2)}, u32[]{:S(2)}) collective-permute-start(f32[584,128]{1,0:T(8,128)S(1)} %get-tuple-element.14), channel_id=1, source_target_pairs={{0,127},{1,0},{2,1},{3,2},{4,3},{5,4},{6,5},{7,6},{8,7},{9,8},{10,... | collective-permute-start | bytes 897032 | tf_op jit(solution)/shard_map/ppermute | solution.py:257

commit v4 on v3

--- a/solution.py
+++ b/solution.py
@@ -4,6 +4,7 @@
 from jax.experimental import pallas as pl
 from jax.experimental.pallas import tpu as pltpu
 from jax.sharding import PartitionSpec as P
+
 
 BLK = 64
 HALF = 6
@@ -123,6 +124,18 @@
                 hi_ref[there], lo_ref[there] = split(tile.T)
 
 
+def spans(side):
+    if side:
+        return slice(0, 2 * LANES), slice(2 * LANES, SUP)
+    return slice(LANES, SUP), slice(0, LANES)
+
+
+def panel_product(side, out_ref, ah, al, bh, bl):
+    w, n = spans(side)
+    out_ref[:, w] = dot3(ah, al, bh[:, w], bl[:, w])
+    out_ref[n, n] = dot3(ah[n, n], al[n, n], bh[n, n], bl[n, n])
+
+
 def local_kernel(pat_ref, x_ref, xh_ref, xl_ref, th_ref, tl_ref, base_ref, part_ref, side_ref, nat_ref, sqh_ref, sql_ref):
     for row in range(ROWS):
         for tile in range(3 * TILES):
@@ -132,27 +145,32 @@
         cols = slice(tile * LANES, (tile + 1) * LANES)
         xh_ref[:, cols], xl_ref[:, cols] = split(nat_ref[tile])
         th_ref[cols, :], tl_ref[cols, :] = split(nat_ref[tile].T)
-    square = dot3(xh_ref[...], xl_ref[...], th_ref[...], tl_ref[...])
-    for row in range(ROWS):
-        rows = slice(row * BLK, (row + 1) * BLK)
-        for tile in range(TILES):
-            cols = slice(tile * LANES, (tile + 1) * LANES)
-            kept = square[rows, cols] * mask_tile(pat_ref, row, TILES + tile)
-            base_ref[rows, cols] = kept
-            sqh_ref[rows, cols], sql_ref[rows, cols] = split(kept)
+    wide, last, used = slice(0, 2 * LANES), slice(2 * LANES, SUP), slice(2 * LANES, 3 * SUP)
+    main = dot3(xh_ref[...], xl_ref[...], th_ref[:, wide], tl_ref[:, wide])
+    own = dot3(xh_ref[last, used], xl_ref[last, used], th_ref[used, last], tl_ref[used, last])
+    for p in range(TILES):
+        for t in range(TILES):
+            cols = slice(t * LANES, (t + 1) * LANES)
+            if t < TILES - 1:
+                square = main[p * LANES : (p + 1) * LANES, cols]
+            else:
+                square = own if p == t else main[last, p * LANES : (p + 1) * LANES].T
+            for row in (2 * p, 2 * p + 1):
+                rows = slice(row * BLK, (row + 1) * BLK)
+                kept = square[row % 2 * BLK : (row % 2 + 1) * BLK] * mask_tile(pat_ref, row, TILES + t)
+                base_ref[rows, cols] = kept
+                sqh_ref[rows, cols], sql_ref[rows, cols] = split(kept)
     dh, dl = xh_ref[:, SUP : 2 * SUP], xl_ref[:, SUP : 2 * SUP]
     for side, first in ((0, 0), (1, 2 * SUP)):
         cols = slice(first, first + SUP)
-        part_ref[side] = dot3(dh, dl, xh_ref[:, cols], xl_ref[:, cols])
-        side_ref[side] = dot3(sqh_ref[...], sql_ref[...], xh_ref[:, cols], xl_ref[:, cols])
+        panel_product(side, part_ref.at[side], dh, dl, xh_ref[:, cols], xl_ref[:, cols])
+        panel_product(side, side_ref.at[side], sqh_ref[...], sql_ref[...], xh_ref[:, cols], xl_ref[:, cols])
     cube = dot3(sqh_ref[...], sql_ref[...], dh, dl)
     base_ref[...] = 3.0 * base_ref[...] - 2.0 * cube
 
 
 def corner_product(side, ah, al, bh, bl):
-    wide, narrow = ((0, 2), (2, 3)) if side else ((1, 3), (0, 1))
-    (w0, w1), (n0, n1) = (tuple(LANES * t for t in span) for span in (wide, narrow))
-    w, n = slice(w0, w1), slice(n0, n1)
+    w, n = spans(side)
     main = dot3(ah[:, w], al[:, w], bh[w, w], bl[w, w])
     extra = dot3(ah[n, n], al[n, n], bh[n, w], bl[n, w])
     own = dot3(ah[n, :], al[n, :], bh[:, n], bl[:, n])
@@ -174,73 +192,77 @@
     return main[rows, lanes]
 
 
-def finish_kernel(
-    pat_ref, prev_ref, next_ref, xh_ref, xl_ref, th_ref, tl_ref, base_ref, part_ref, side_ref,
-    out_hbm, dh_ref, dl_ref, eh_ref, el_ref, nat_ref, out_ref, sems,
-):
-    for side, rec_ref in ((0, prev_ref), (1, next_ref)):
-        unpack_split(rec_ref, dh_ref.at[side], dl_ref.at[side])
-    for side in (0, 1):
-        cols = slice(2 * side * SUP, (2 * side + 1) * SUP)
-        parts = corner_product(side, xh_ref[:, cols], xl_ref[:, cols], dh_ref[side], dl_ref[side])
-        for p in range(TILES):
-            for t in range(TILES):
-                edge = corner_tile(side, parts, p, t)
-                lanes = slice(side * SUP + t * LANES, side * SUP + (t + 1) * LANES)
-                tile = 2 * side * TILES + t
-                if edge is None:
-                    nothing = jnp.zeros((LANES, LANES), BF16)
-                    eh_ref[p * LANES : (p + 1) * LANES, lanes] = nothing
-                    el_ref[p * LANES : (p + 1) * LANES, lanes] = nothing
-                    continue
-                edge = edge + part_ref[side, p * LANES : (p + 1) * LANES, t * LANES : (t + 1) * LANES]
-                for row in (2 * p, 2 * p + 1):
-                    rows = slice(row * BLK, (row + 1) * BLK)
-                    kept = edge[row % 2 * BLK : (row % 2 + 1) * BLK] * mask_tile(pat_ref, row, tile)
-                    nat_ref[tile, rows, :] = 3.0 * kept
-                    eh_ref[rows, lanes], el_ref[rows, lanes] = split(kept)
-    wide0, narrow0 = slice(LANES, SUP), slice(0, LANES)
-    wide1, narrow1 = slice(0, 2 * LANES), slice(2 * LANES, SUP)
-    eh, el = (ref[:, :SUP] for ref in (eh_ref, el_ref))
-    fh, fl = (ref[:, SUP:] for ref in (eh_ref, el_ref))
-    lh, ll = (ref[:SUP, :] for ref in (th_ref, tl_ref))
-    uh, ul = (ref[2 * SUP :, :] for ref in (th_ref, tl_ref))
-    main = dot3(
-        jnp.concatenate([eh[:, wide0], fh[:, wide1]], 1),
-        jnp.concatenate([el[:, wide0], fl[:, wide1]], 1),
-        jnp.concatenate([lh[wide0, :], uh[wide1, :]], 0),
-        jnp.concatenate([ll[wide0, :], ul[wide1, :]], 0),
-    )
-    first = dot3(eh[narrow0, narrow0], el[narrow0, narrow0], lh[narrow0, narrow0], ll[narrow0, narrow0])
-    last = dot3(fh[narrow1, narrow1], fl[narrow1, narrow1], uh[narrow1, narrow1], ul[narrow1, narrow1])
+def one_side(side, pat_ref, rec_ref, x_refs, t_refs, base_ref, part_ref, side_ref, nat_ref, sum_ref, d_refs, e_refs):
+    (xh_ref, xl_ref), (th_ref, tl_ref), (dh_ref, dl_ref), (eh_ref, el_ref) = x_refs, t_refs, d_refs, e_refs
+    unpack_split(rec_ref, dh_ref, dl_ref)
+    panel = slice(2 * side * SUP, (2 * side + 1) * SUP)
+    far = TILES - 1 if side else 0
+    parts = corner_product(side, xh_ref[:, panel], xl_ref[:, panel], dh_ref, dl_ref)
+    for p in range(TILES):
+        rows = slice(p * LANES, (p + 1) * LANES)
+        for t in range(TILES):
+            edge = corner_tile(side, parts, p, t)
+            lanes = slice(t * LANES, (t + 1) * LANES)
+            if edge is None:
+                nothing = jnp.zeros((LANES, LANES), BF16)
+                eh_ref[rows, lanes], el_ref[rows, lanes] = nothing, nothing
+                nat_ref[t, rows, :] = jnp.zeros((LANES, LANES), F32)
+                continue
+            edge = edge + part_ref[side, rows, lanes]
+            for row in (2 * p, 2 * p + 1):
+                half = slice(row * BLK, (row + 1) * BLK)
+                kept = edge[row % 2 * BLK : (row % 2 + 1) * BLK] * mask_tile(pat_ref, row, 2 * side * TILES + t)
+                nat_ref[t, half, :] = 3.0 * kept
+                eh_ref[half, lanes], el_ref[half, lanes] = split(kept)
+    w, n = spans(side)
+    bh, bl = th_ref[panel, :], tl_ref[panel, :]
+    main = dot3(eh_ref[:, w], el_ref[:, w], bh[w, :], bl[w, :])
+    own = dot3(eh_ref[n, n], el_ref[n, n], bh[n, n], bl[n, n])
     for p in range(TILES):
         rows = slice(p * LANES, (p + 1) * LANES)
         for t in range(TILES):
             lanes = slice(t * LANES, (t + 1) * LANES)
             cube = main[rows, lanes]
-            if p == t == 0:
-                cube = cube + first
-            if p == t == TILES - 1:
-                cube = cube + last
-            nat_ref[TILES + t, rows, :] = base_ref[rows, lanes] - 2.0 * cube
-    for side in (0, 1):
-        cols = slice(side * SUP, (side + 1) * SUP)
-        parts = corner_product(side, eh_ref[:, cols], el_ref[:, cols], dh_ref[side], dl_ref[side])
-        for p in range(TILES):
-            rows = slice(p * LANES, (p + 1) * LANES)
-            for t in range(TILES):
-                cube = corner_tile(side, parts, p, t)
-                if cube is None:
-                    continue
-                tile = 2 * side * TILES + t
+            if p == t == far:
+                cube = cube + own
+            sum_ref[rows, lanes] = base_ref[rows, lanes] - 2.0 * cube
+    parts = corner_product(side, eh_ref, el_ref, dh_ref, dl_ref)
+    for p in range(TILES):
+        rows = slice(p * LANES, (p + 1) * LANES)
+        for t in range(TILES):
+            cube = corner_tile(side, parts, p, t)
+            if cube is not None:
                 cube = cube + side_ref[side, rows, t * LANES : (t + 1) * LANES]
-                nat_ref[tile, rows, :] = nat_ref[tile, rows, :] - 2.0 * cube
+                nat_ref[t, rows, :] = nat_ref[t, rows, :] - 2.0 * cube
+
+
+def next_kernel(
+    pat_ref, rec_ref, xh_ref, xl_ref, th_ref, tl_ref, base_ref, part_ref, side_ref,
+    nat_ref, sum_ref, dh_ref, dl_ref, eh_ref, el_ref,
+):
+    one_side(
+        1, pat_ref, rec_ref, (xh_ref, xl_ref), (th_ref, tl_ref), base_ref, part_ref, side_ref,
+        nat_ref, sum_ref, (dh_ref, dl_ref), (eh_ref, el_ref),
+    )
+
+
+def prev_kernel(
+    pat_ref, rec_ref, xh_ref, xl_ref, th_ref, tl_ref, base_ref, part_ref, side_ref, right_ref,
+    out_hbm, left_ref, sum_ref, mid_ref, dh_ref, dl_ref, eh_ref, el_ref, out_ref, sems,
+):
+    one_side(
+        0, pat_ref, rec_ref, (xh_ref, xl_ref), (th_ref, tl_ref), base_ref, part_ref, side_ref,
+        left_ref, sum_ref, (dh_ref, dl_ref), (eh_ref, el_ref),
+    )
+    for t in range(TILES):
+        mid_ref[t] = sum_ref[:, t * LANES : (t + 1) * LANES]
     copies = []
     for row in range(ROWS):
         for tile in range(row // 2, (row + SLOTS - 1) // 2 + 1):
+            nat_ref = (left_ref, mid_ref, right_ref)[tile // TILES]
             mask = mask_tile(pat_ref, row, tile)
-            even = nat_ref[tile, pl.ds(row * BLK, BLK // 2, stride=2), :] * mask
-            odd = nat_ref[tile, pl.ds(row * BLK + 1, BLK // 2, stride=2), :] * mask
+            even = nat_ref[tile % TILES, pl.ds(row * BLK, BLK // 2, stride=2), :] * mask
+            odd = nat_ref[tile % TILES, pl.ds(row * BLK + 1, BLK // 2, stride=2), :] * mask
             left, right = even_odd_rows(even, odd)
             for slot, block in ((2 * tile - row, left), (2 * tile + 1 - row, right)):
                 if 0 <= slot < SLOTS:
@@ -274,8 +296,8 @@
         scratch_shapes=[pltpu.SemaphoreType.DMA((ROWS,))],
     )(pltpu.with_memory_space_constraint(density, pltpu.HBM))
     density = on_chip(density)
+    prev = from_behind(packed, 1)
     following = from_behind(packed, -1)
-    prev = from_behind(packed, 1)
     local = pl.pallas_call(
         local_kernel,
         name="local",
@@ -297,23 +319,34 @@
             pltpu.VMEM((SUP, SUP), BF16),
         ],
     )(pattern, density)
+    *x_and_t, base, part, side = (on_chip(x) for x in local)
+    work = [pltpu.VMEM((SUP, SUP), BF16) for _ in range(4)]
+    strip = (TILES, SUP, LANES)
+    right, base = pl.pallas_call(
+        next_kernel,
+        name="next_side",
+        compiler_params=SMALL,
+        in_specs=[smem] + [vmem] * 8,
+        out_specs=[vmem] * 2,
+        out_shape=[pltpu.VMEM(strip, F32), pltpu.VMEM((SUP, SUP), F32)],
+        scratch_shapes=work,
+    )(pattern, on_chip(following), *x_and_t, base, part, side)
     return pl.pallas_call(
-        finish_kernel,
-        name="finish",
+        prev_kernel,
+        name="prev_side",
         compiler_params=SMALL,
         in_specs=[smem] + [vmem] * 9,
         out_specs=pl.BlockSpec(memory_space=pltpu.HBM),
         out_shape=jax.ShapeDtypeStruct((ROWS, SLOTS, BLK * BLK), F32),
         scratch_shapes=[
-            pltpu.VMEM((2, SUP, SUP), BF16),
-            pltpu.VMEM((2, SUP, SUP), BF16),
-            pltpu.VMEM((SUP, 2 * SUP), BF16),
-            pltpu.VMEM((SUP, 2 * SUP), BF16),
-            pltpu.VMEM((3 * TILES, SUP, LANES), F32),
+            pltpu.VMEM(strip, F32),
+            pltpu.VMEM((SUP, SUP), F32),
+            pltpu.VMEM(strip, F32),
+            *work,
             pltpu.VMEM((ROWS, SLOTS, BLK * BLK), F32),
             pltpu.SemaphoreType.DMA((ROWS,)),
         ],
-    )(pattern, *(on_chip(x) for x in (prev, following, *local)))
+    )(pattern, on_chip(prev), *x_and_t, on_chip(base), part, side, on_chip(right))
 
 
 def solution(mesh):

time: 21.1 us -> 25.2 us (1.19)
  the two profiles are of different devices: /device:TPU:1 before, /device:TPU:0 now
where the time goes in v4:
time: 25.2 us; the launch traced here: 25.1 us
  Pallas kernels  12 us (48%)
  starting transfers between devices  8.31 us (33%)
  waiting for transfers between devices  4.8 us (19%)
    ppermute x2, starting transfers between devices, from_behind(): lax.ppermute(x, axes, [(i, (i + by) % length) for i in range(length)])  8.31 us
    ppermute x2, waiting for transfers between devices, from_behind(): lax.ppermute(x, axes, [(i, (i + by) % length) for i in range(length)])  4.8 us
    pallas_call x1, Pallas kernels, shards(): pl.pallas_call(local_kernel, name='local', compiler_params=SMALL, in_spec...  4.61 us
    pallas_call x1, Pallas kernels, shards(): pl.pallas_call(prev_kernel, name='prev_side', compiler_params=SMALL, in_s...  3.62 us
    pallas_call x1, Pallas kernels, shards(): pl.pallas_call(next_kernel, name='next_side', compiler_params=SMALL, in_s...  2.18 us
    pallas_call x1, Pallas kernels, shards(): pl.pallas_call(pack_kernel, name='pack', compiler_params=SMALL, in_specs=...  1.57 us
  transfers between devices with their start and end apart: 2, of which 1 were waited for; matrix products, arithmetic and copies ran while one was open for 0% of the time, Pallas kernels for 27%

profile of v4, /device:TPU:0, one launch (start us, length us, event | category | flops | bytes accessed | tf_op | source)
XLA Modules:
  0.0 25.1 jit_solution(12439656931154522014)
XLA Ops:
  0.0 0.0 copy-start
  0.0 1.6 %pack.1 = (f32[584,128]{1,0:T(8,128)S(1)}, f32[6,13,4096]{2,1,0:T(8,128)S(1)}) custom-call(f32[6,13,4096]{2,1,0:T(8,128)} %hbm_ref.1), custom_call_target="tpu_custom_call" | custom-call | tf_op jit(solution)/shard_map/pack/pallas_call | solution.py:289
  1.6 8.3 %collective-permute-start.1 = (f32[584,128]{1,0:T(8,128)S(1)}, f32[584,128]{1,0:T(8,128)S(1)}, u32[]{:S(2)}, u32[]{:S(2)}) collective-permute-start(f32[584,128]{1,0:T(8,128)S(1)} %get-tuple-element.16), channel_id=1, source_target_pairs={{0,127},{1,0},{2,1},{3,2},{4,3},{5,4},{6,5},{7,6},{8,7},{9,8},{10,... | collective-permute-start | bytes 897032 | tf_op jit(solution)/shard_map/ppermute | solution.py:279
  9.9 0.0 collective-permute-start
  9.9 0.0 copy-done
  9.9 4.6 %local.1 = (bf16[384,1152]{1,0:T(8,128)(2,1)S(1)}, bf16[384,1152]{1,0:T(8,128)(2,1)S(1)}, bf16[1152,384]{1,0:T(8,128)(2,1)S(1)}, bf16[1152,384]{1,0:T(8,128)(2,1...) custom-call(s32[6,13]{1,0:T(8,128)S(1)} %copy-done, ...), custom_call_target="tpu_custom_call" | custom-call | tf_op jit(solution)/shard_map/local/pallas_call | solution.py:301
  14.5 0.0 collective-permute-done.1.rec_ref
  14.5 2.2 %next_side.1 = (f32[3,384,128]{2,1,0:T(8,128)S(1)}, f32[384,384]{1,0:T(8,128)S(1)}) custom-call(s32[6,13]{1,0:T(8,128)S(1)} %copy-done, f32[584,128]{1,0:T(8,128)S(1)} %collective-permute-done.1.rec_ref, bf16[384,1152]{1,0:T(8,128)(2,1)S(1)} %get-tuple-element.18.xh_ref, bf16[384,1152]{1,0:T(8,128)(2,1)S(1)} %get-tuple-element.19.xl_ref, ...), custom_call_target="tpu_custom_call" | custom-call | tf_op jit(solution)/shard_map/next_side/pallas_call | solution.py:325
  16.7 4.8 %collective-permute-done.rec_ref = f32[584,128]{1,0:T(8,128)S(1)} collective-permute-done((f32[584,128]{1,0:T(8,128)S(1)}, f32[584,128]{1,0:T(8,128)S(1)}, u32[]{:S(2)}, u32[]{:S(2)}) %collective-permute-start) | collective-permute-done | bytes 299040 | tf_op jit(solution)/shard_map/ppermute | solution.py:279
  21.5 3.6 %prev_side.1 = f32[6,13,4096]{2,1,0:T(8,128)} custom-call(s32[6,13]{1,0:T(8,128)S(1)} %copy-done, f32[584,128]{1,0:T(8,128)S(1)} %collective-permute-done.rec_ref, bf16[384,1152]{1,0:T(8,128)(2,1)S(1)} %get-tuple-element.18.xh_ref, bf16[384,1152]{1,0:T(8,128)(2,1)S(1)} %get-tuple-element.19.xl_ref, bf16[1152,384]{1,0:T(8,128)(2,1)S(1)} %get-tuple-element.20.th_ref, ...), custom_call_target="tpu_custom_call" | custom-call | tf_op jit(solution)/shard_map/prev_side/pallas_call | solution.py:334
Async XLA Ops:
  0.0 9.9 %copy-start = (s32[6,13]{1,0:T(8,128)S(1)}, s32[6,13]{1,0:T(8,128)}, u32[]{:S(2)}) copy-start(s32[6,13]{1,0:T(8,128)} %pat_ref.5) | copy-start | bytes 940
  1.6 12.9 %collective-permute-start.1 = (f32[584,128]{1,0:T(8,128)S(1)}, f32[584,128]{1,0:T(8,128)S(1)}, u32[]{:S(2)}, u32[]{:S(2)}) collective-permute-start(f32[584,128]{1,0:T(8,128)S(1)} %get-tuple-element.16), channel_id=1, source_target_pairs={{0,127},{1,0},{2,1},{3,2},{4,3},{5,4},{6,5},{7,6},{8,7},{9,8},{10,... | collective-permute-start | bytes 897032 | tf_op jit(solution)/shard_map/ppermute | solution.py:279
  9.9 11.6 %collective-permute-start = (f32[584,128]{1,0:T(8,128)S(1)}, f32[584,128]{1,0:T(8,128)S(1)}, u32[]{:S(2)}, u32[]{:S(2)}) collective-permute-start(f32[584,128]{1,0:T(8,128)S(1)} %get-tuple-element.16), channel_id=1, source_target_pairs={{0,1},{1,2},{2,3},{3,4},{4,5},{5,6},{6,7},{7,8},{8,9},{9,10},{10,1... | collective-permute-start | bytes 897032 | tf_op jit(solution)/shard_map/ppermute | solution.py:279

commit v5 on v3

--- a/solution.py
+++ b/solution.py
@@ -123,6 +123,18 @@
                 hi_ref[there], lo_ref[there] = split(tile.T)
 
 
+def spans(side):
+    if side:
+        return slice(0, 2 * LANES), slice(2 * LANES, SUP)
+    return slice(LANES, SUP), slice(0, LANES)
+
+
+def panel_product(side, out_ref, ah, al, bh, bl):
+    w, n = spans(side)
+    out_ref[:, w] = dot3(ah, al, bh[:, w], bl[:, w])
+    out_ref[n, n] = dot3(ah[n, n], al[n, n], bh[n, n], bl[n, n])
+
+
 def local_kernel(pat_ref, x_ref, xh_ref, xl_ref, th_ref, tl_ref, base_ref, part_ref, side_ref, nat_ref, sqh_ref, sql_ref):
     for row in range(ROWS):
         for tile in range(3 * TILES):
@@ -132,27 +144,32 @@
         cols = slice(tile * LANES, (tile + 1) * LANES)
         xh_ref[:, cols], xl_ref[:, cols] = split(nat_ref[tile])
         th_ref[cols, :], tl_ref[cols, :] = split(nat_ref[tile].T)
-    square = dot3(xh_ref[...], xl_ref[...], th_ref[...], tl_ref[...])
-    for row in range(ROWS):
-        rows = slice(row * BLK, (row + 1) * BLK)
-        for tile in range(TILES):
-            cols = slice(tile * LANES, (tile + 1) * LANES)
-            kept = square[rows, cols] * mask_tile(pat_ref, row, TILES + tile)
-            base_ref[rows, cols] = kept
-            sqh_ref[rows, cols], sql_ref[rows, cols] = split(kept)
+    wide, last, used = slice(0, 2 * LANES), slice(2 * LANES, SUP), slice(2 * LANES, 3 * SUP)
+    main = dot3(xh_ref[...], xl_ref[...], th_ref[:, wide], tl_ref[:, wide])
+    own = dot3(xh_ref[last, used], xl_ref[last, used], th_ref[used, last], tl_ref[used, last])
+    for p in range(TILES):
+        for t in range(TILES):
+            cols = slice(t * LANES, (t + 1) * LANES)
+            if t < TILES - 1:
+                square = main[p * LANES : (p + 1) * LANES, cols]
+            else:
+                square = own if p == t else main[last, p * LANES : (p + 1) * LANES].T
+            for row in (2 * p, 2 * p + 1):
+                rows = slice(row * BLK, (row + 1) * BLK)
+                kept = square[row % 2 * BLK : (row % 2 + 1) * BLK] * mask_tile(pat_ref, row, TILES + t)
+                base_ref[rows, cols] = kept
+                sqh_ref[rows, cols], sql_ref[rows, cols] = split(kept)
     dh, dl = xh_ref[:, SUP : 2 * SUP], xl_ref[:, SUP : 2 * SUP]
     for side, first in ((0, 0), (1, 2 * SUP)):
         cols = slice(first, first + SUP)
-        part_ref[side] = dot3(dh, dl, xh_ref[:, cols], xl_ref[:, cols])
-        side_ref[side] = dot3(sqh_ref[...], sql_ref[...], xh_ref[:, cols], xl_ref[:, cols])
+        panel_product(side, part_ref.at[side], dh, dl, xh_ref[:, cols], xl_ref[:, cols])
+        panel_product(side, side_ref.at[side], sqh_ref[...], sql_ref[...], xh_ref[:, cols], xl_ref[:, cols])
     cube = dot3(sqh_ref[...], sql_ref[...], dh, dl)
     base_ref[...] = 3.0 * base_ref[...] - 2.0 * cube
 
 
 def corner_product(side, ah, al, bh, bl):
-    wide, narrow = ((0, 2), (2, 3)) if side else ((1, 3), (0, 1))
-    (w0, w1), (n0, n1) = (tuple(LANES * t for t in span) for span in (wide, narrow))
-    w, n = slice(w0, w1), slice(n0, n1)
+    w, n = spans(side)
     main = dot3(ah[:, w], al[:, w], bh[w, w], bl[w, w])
     extra = dot3(ah[n, n], al[n, n], bh[n, w], bl[n, w])
     own = dot3(ah[n, :], al[n, :], bh[:, n], bl[:, n])
@@ -172,6 +189,20 @@
     if p == far:
         return main[rows, lanes] + extra[:, lanes]
     return main[rows, lanes]
+
+
+def write_tiles(pat_ref, nat_ref, out_ref, panel):
+    for row in range(ROWS):
+        for tile in range(panel * TILES, (panel + 1) * TILES):
+            slots = (2 * tile - row, 2 * tile + 1 - row)
+            if slots[1] < 0 or slots[0] >= SLOTS:
+                continue
+            mask = mask_tile(pat_ref, row, tile)
+            even = nat_ref[tile, pl.ds(row * BLK, BLK // 2, stride=2), :] * mask
+            odd = nat_ref[tile, pl.ds(row * BLK + 1, BLK // 2, stride=2), :] * mask
+            for slot, block in zip(slots, even_odd_rows(even, odd)):
+                if 0 <= slot < SLOTS:
+                    out_ref[row, slot, :] = block.reshape(BLK * BLK)
 
 
 def finish_kernel(
@@ -223,6 +254,9 @@
             if p == t == TILES - 1:
                 cube = cube + last
             nat_ref[TILES + t, rows, :] = base_ref[rows, lanes] - 2.0 * cube
+    write_tiles(pat_ref, nat_ref, out_ref, 1)
+    early = [pltpu.make_async_copy(out_ref.at[row, :8], out_hbm.at[row, :8], sems.at[row, 0]) for row in range(ROWS)]
+    late = [pltpu.make_async_copy(out_ref.at[row, 8:], out_hbm.at[row, 8:], sems.at[row, 1]) for row in range(ROWS)]
     for side in (0, 1):
         cols = slice(side * SUP, (side + 1) * SUP)
         parts = corner_product(side, eh_ref[:, cols], el_ref[:, cols], dh_ref[side], dl_ref[side])
@@ -235,19 +269,13 @@
                 tile = 2 * side * TILES + t
                 cube = cube + side_ref[side, rows, t * LANES : (t + 1) * LANES]
                 nat_ref[tile, rows, :] = nat_ref[tile, rows, :] - 2.0 * cube
-    copies = []
-    for row in range(ROWS):
-        for tile in range(row // 2, (row + SLOTS - 1) // 2 + 1):
-            mask = mask_tile(pat_ref, row, tile)
-            even = nat_ref[tile, pl.ds(row * BLK, BLK // 2, stride=2), :] * mask
-            odd = nat_ref[tile, pl.ds(row * BLK + 1, BLK // 2, stride=2), :] * mask
-            left, right = even_odd_rows(even, odd)
-            for slot, block in ((2 * tile - row, left), (2 * tile + 1 - row, right)):
-                if 0 <= slot < SLOTS:
-                    out_ref[row, slot, :] = block.reshape(BLK * BLK)
-        copies.append(pltpu.make_async_copy(out_ref.at[row], out_hbm.at[row], sems.at[row]))
-        copies[-1].start()
-    for copy in copies:
+        write_tiles(pat_ref, nat_ref, out_ref, 2 * side)
+        if side == 0:
+            for copy in early[:-1]:
+                copy.start()
+    for copy in (early[-1], *late):
+        copy.start()
+    for copy in (*early, *late):
         copy.wait()
 
 
@@ -311,7 +339,7 @@
             pltpu.VMEM((SUP, 2 * SUP), BF16),
             pltpu.VMEM((3 * TILES, SUP, LANES), F32),
             pltpu.VMEM((ROWS, SLOTS, BLK * BLK), F32),
-            pltpu.SemaphoreType.DMA((ROWS,)),
+            pltpu.SemaphoreType.DMA((ROWS, 2)),
         ],
     )(pattern, *(on_chip(x) for x in (prev, following, *local)))
 

time: 21.1 us -> 21.2 us (level)
  waiting for transfers between devices: 2.1 us -> 2.91 us
  Pallas kernels: 11.1 us -> 10.4 us
    pallas_call x1, Pallas kernels: 5.47 us -> 4.66 us  [shards(): pl.pallas_call(local_kernel, name='local', compiler_params=SMALL, in_spec...]
    ppermute x2, waiting for transfers between devices: 2.1 us -> 2.91 us  [from_behind(): lax.ppermute(x, axes, [(i, (i + by) % length) for i in range(length)])]
  transfers between devices with their start and end apart: 2 -> 2, of which waited for: 1 -> 1; matrix products, arithmetic and copies ran while one was open for 0% -> 0% of each run, Pallas kernels for 26% -> 22%
where the time goes in v5:
time: 21.2 us; the launch traced here: 21.1 us
  Pallas kernels  10.4 us (49%)
  starting transfers between devices  7.74 us (37%)
  waiting for transfers between devices  2.91 us (14%)
    ppermute x2, starting transfers between devices, from_behind(): lax.ppermute(x, axes, [(i, (i + by) % length) for i in range(length)])  7.74 us
    pallas_call x1, Pallas kernels, shards(): pl.pallas_call(local_kernel, name='local', compiler_params=SMALL, in_spec...  4.66 us
    pallas_call x1, Pallas kernels, shards(): pl.pallas_call(finish_kernel, name='finish', compiler_params=SMALL, in_sp...  4.16 us
    ppermute x2, waiting for transfers between devices, from_behind(): lax.ppermute(x, axes, [(i, (i + by) % length) for i in range(length)])  2.91 us
    pallas_call x1, Pallas kernels, shards(): pl.pallas_call(pack_kernel, name='pack', compiler_params=SMALL, in_specs=...  1.57 us
  transfers between devices with their start and end apart: 2, of which 1 were waited for; matrix products, arithmetic and copies ran while one was open for 0% of the time, Pallas kernels for 22%

profile of v5, /device:TPU:1, one launch (start us, length us, event | category | flops | bytes accessed | tf_op | source)
XLA Modules:
  0.0 21.1 jit_solution(3084383000353972300)
XLA Ops:
  0.0 0.0 copy-start
  0.0 1.6 %pack.1 = (f32[584,128]{1,0:T(8,128)S(1)}, f32[6,13,4096]{2,1,0:T(8,128)S(1)}) custom-call(f32[6,13,4096]{2,1,0:T(8,128)} %hbm_ref.1), custom_call_target="tpu_custom_call" | custom-call | tf_op jit(solution)/shard_map/pack/pallas_call | solution.py:295
  1.6 2.5 %collective-permute-start = (f32[584,128]{1,0:T(8,128)S(1)}, f32[584,128]{1,0:T(8,128)S(1)}, u32[]{:S(2)}, u32[]{:S(2)}) collective-permute-start(f32[584,128]{1,0:T(8,128)S(1)} %get-tuple-element.14), channel_id=1, source_target_pairs={{0,1},{1,2},{2,3},{3,4},{4,5},{5,6},{6,7},{7,8},{8,9},{9,10},{10,1... | collective-permute-start | bytes 897032 | tf_op jit(solution)/shard_map/ppermute | solution.py:285
  4.1 5.2 %collective-permute-start.1 = (f32[584,128]{1,0:T(8,128)S(1)}, f32[584,128]{1,0:T(8,128)S(1)}, u32[]{:S(2)}, u32[]{:S(2)}) collective-permute-start(f32[584,128]{1,0:T(8,128)S(1)} %get-tuple-element.14), channel_id=1, source_target_pairs={{0,127},{1,0},{2,1},{3,2},{4,3},{5,4},{6,5},{7,6},{8,7},{9,8},{10,... | collective-permute-start | bytes 897032 | tf_op jit(solution)/shard_map/ppermute | solution.py:285
  9.3 0.0 copy-done
  9.3 4.7 %local.1 = (bf16[384,1152]{1,0:T(8,128)(2,1)S(1)}, bf16[384,1152]{1,0:T(8,128)(2,1)S(1)}, bf16[1152,384]{1,0:T(8,128)(2,1)S(1)}, bf16[1152,384]{1,0:T(8,128)(2,1...) custom-call(s32[6,13]{1,0:T(8,128)S(1)} %copy-done, ...), custom_call_target="tpu_custom_call" | custom-call | tf_op jit(solution)/shard_map/local/pallas_call | solution.py:307
  14.0 2.9 %collective-permute-done.prev_ref = f32[584,128]{1,0:T(8,128)S(1)} collective-permute-done((f32[584,128]{1,0:T(8,128)S(1)}, f32[584,128]{1,0:T(8,128)S(1)}, u32[]{:S(2)}, u32[]{:S(2)}) %collective-permute-start) | collective-permute-done | bytes 299040 | tf_op jit(solution)/shard_map/ppermute | solution.py:285
  16.9 0.0 collective-permute-done.1.next_ref
  16.9 4.2 %finish.1 = f32[6,13,4096]{2,1,0:T(8,128)} custom-call(s32[6,13]{1,0:T(8,128)S(1)} %copy-done, f32[584,128]{1,0:T(8,128)S(1)} %collective-permute-done.prev_ref, f32[584,128]{1,0:T(8,128)S(1)} %collective-permute-done.1.next_ref, bf16[384,1152]{1,0:T(8,128)(2,1)S(1)} %get-tuple-element.16.xh_ref, bf16[384,1152]{1,0:T(8,128)(2,1)S(1)} %get-tuple-element.17.xl_ref, ...), custom_call_target="tpu_custom_call" | custom-call | tf_op jit(solution)/shard_map/finish/pallas_call | solution.py:328
Async XLA Ops:
  0.0 9.3 %copy-start = (s32[6,13]{1,0:T(8,128)S(1)}, s32[6,13]{1,0:T(8,128)}, u32[]{:S(2)}) copy-start(s32[6,13]{1,0:T(8,128)} %pat_ref.3) | copy-start | bytes 940
  1.6 15.3 %collective-permute-start = (f32[584,128]{1,0:T(8,128)S(1)}, f32[584,128]{1,0:T(8,128)S(1)}, u32[]{:S(2)}, u32[]{:S(2)}) collective-permute-start(f32[584,128]{1,0:T(8,128)S(1)} %get-tuple-element.14), channel_id=1, source_target_pairs={{0,1},{1,2},{2,3},{3,4},{4,5},{5,6},{6,7},{7,8},{8,9},{9,10},{10,1... | collective-permute-start | bytes 897032 | tf_op jit(solution)/shard_map/ppermute | solution.py:285
  4.1 12.8 %collective-permute-start.1 = (f32[584,128]{1,0:T(8,128)S(1)}, f32[584,128]{1,0:T(8,128)S(1)}, u32[]{:S(2)}, u32[]{:S(2)}) collective-permute-start(f32[584,128]{1,0:T(8,128)S(1)} %get-tuple-element.14), channel_id=1, source_target_pairs={{0,127},{1,0},{2,1},{3,2},{4,3},{5,4},{6,5},{7,6},{8,7},{9,8},{10,... | collective-permute-start | bytes 897032 | tf_op jit(solution)/shard_map/ppermute | solution.py:285
